TPU v7x, 256 devices: a whole 4x4x8 slice. The times are simulated.
256 devices in a mesh: member: 8 (over z_hi, core), lat: 32 (over y, z_lo, x).
Axes of the slice: x: 4, y: 4, z: 8 (z_hi: 4, z_lo: 2; z = z_hi * 2 + z_lo), core: 2. Of those that a mesh axis runs over, the one named last changes fastest.
Arguments:
- ensemble: bfloat16 [16, 64, 128, 256], P('member', None, 'lat'), may hold values from -6 to 6
- cotangent: bfloat16 [16, 64, 128, 256], P('member', None, 'lat'), may hold values from -6 to 6
- conv_in: bfloat16 [3, 3, 64, 128], replicated, may hold values from -0.25 to 0.25
- pool_weight: bfloat16 [256, 128], replicated, may hold values from -1 to 1
- conv_out: bfloat16 [3, 3, 128, 64], replicated, may hold values from -0.1875 to 0.1875
Outputs:
- encoded: bfloat16 [16, 64, 128, 256], P('member', None, 'lat')
- d_input: bfloat16 [16, 64, 128, 256], P('member', None, 'lat')
- grad_conv_in: float32 [3, 3, 64, 128], replicated
- grad_pool: float32 [256, 128], replicated
- grad_conv_out: float32 [3, 3, 128, 64], replicated
All inputs are finite; a program needn't handle non-finite values.
Results may differ from a plain program's by a relative error of at most 0.0085.
Values may be sent and summed in bfloat16 or wider, within the bound.
No kernel may reach another device: no remote copies, remote signals or barrier semaphores. Data moves between devices by JAX's collectives and lax.ppermute only.
A program may use at most 64 MiB of HBM per device.

v0:
```python
import math
import jax
import jax.numpy as jnp
from jax import lax
from jax.sharding import PartitionSpec as P


def padded(cells, sides, width):
    for axis, dim in sides:
        count = lax.axis_size(axis)
        ends = count - 1
        head = lax.slice_in_dim(cells, 0, width, axis=dim)
        tail = lax.slice_in_dim(cells, cells.shape[dim] - width, cells.shape[dim], axis=dim)
        cells = jnp.concatenate(
            [
                lax.ppermute(tail, axis, [(i, (i + 1) % count) for i in range(ends)]),
                cells,
                lax.ppermute(head, axis, [((i + 1) % count, i) for i in range(ends)]),
            ],
            axis=dim,
        )
    return cells


def wrap_longitude(field):
    return jnp.concatenate([field[..., -1:], field, field[..., :1]], axis=3)


def convolve(padded_rows, kernel):
    return lax.conv_general_dilated(
        wrap_longitude(padded_rows),
        kernel,
        (1, 1),
        "VALID",
        dimension_numbers=("NCHW", "HWIO", "NCHW"),
        preferred_element_type=jnp.float32,
    )


def flipped(kernel):
    return jnp.transpose(kernel[::-1, ::-1], (0, 1, 3, 2))


def kernel_grad(padded_rows, output_grad):
    return lax.conv_general_dilated(
        wrap_longitude(padded_rows),
        output_grad,
        (1, 1),
        "VALID",
        dimension_numbers=("CNHW", "IOHW", "HWNC"),
        preferred_element_type=jnp.float32,
    )


def silu_slope(values):
    sigma = jax.nn.sigmoid(values)
    return sigma * (1.0 + values * (1.0 - sigma))


def on_device(ensemble, cotangent, conv_in, pool_weight, conv_out):
    mem_local, var_count, lat_local, lon_count = ensemble.shape
    groups = lax.axis_size("member")
    members = mem_local * groups
    cell_count = lat_local * lon_count
    ens_rows = padded(ensemble, (("lat", 2),), 1)
    pre = convolve(ens_rows, conv_in)
    active = jax.nn.silu(pre).astype(jnp.bfloat16)
    channels = active.shape[1]
    active_cells = active.reshape(mem_local, channels, cell_count)
    active_wide = active_cells.astype(jnp.float32)
    pool_wide = pool_weight.astype(jnp.float32)
    grouped = lax.all_to_all(
        active_cells, "member", split_axis=2, concat_axis=0, tiled=True
    ).astype(jnp.float32)
    local_average = jnp.mean(grouped, axis=0)
    local_spread = jnp.sqrt(jnp.mean((grouped - local_average) ** 2, axis=0) + 0.1)
    local_stats = jnp.concatenate([local_average, local_spread], axis=0)
    local_shared = jnp.dot(pool_wide.T, local_stats, precision=lax.Precision.HIGHEST)
    shared, average, spread = (
        lax.all_gather(local_shared, "member", axis=1, tiled=True),
        lax.all_gather(local_average, "member", axis=1, tiled=True),
        lax.all_gather(local_spread, "member", axis=1, tiled=True),
    )
    zed = active_wide + shared
    hidden = (
        jax.nn.silu(zed).astype(jnp.bfloat16).reshape(mem_local, channels, lat_local, lon_count)
    )
    hid_rows = padded(hidden, (("lat", 2),), 1)
    encoded = (ensemble.astype(jnp.float32) + convolve(hid_rows, conv_out)).astype(jnp.bfloat16)
    cot_rows = padded(cotangent, (("lat", 2),), 1)
    d_hidden = convolve(cot_rows, flipped(conv_out)).reshape(mem_local, channels, cell_count)
    d_zed = (d_hidden * silu_slope(zed)).astype(jnp.bfloat16)
    grad_out = kernel_grad(hid_rows, cotangent)
    zed_grouped = lax.all_to_all(d_zed, "member", split_axis=2, concat_axis=0, tiled=True)
    local_dshared = jnp.sum(zed_grouped.astype(jnp.float32), axis=0)
    local_dstats = jnp.dot(pool_wide, local_dshared, precision=lax.Precision.HIGHEST)
    grad_pool = jnp.dot(local_stats, local_dshared.T, precision=lax.Precision.HIGHEST)
    coef_average = local_dstats[:channels] / members
    coef_spread = local_dstats[channels:] / (members * local_spread)
    coef_average, coef_spread = (
        lax.all_gather(coef_average.astype(jnp.bfloat16), "member", axis=1, tiled=True).astype(
            coef_average.dtype
        ),
        lax.all_gather(coef_spread.astype(jnp.bfloat16), "member", axis=1, tiled=True).astype(
            coef_spread.dtype
        ),
    )
    d_active = d_zed.astype(jnp.float32) + coef_average + coef_spread * (active_wide - average)
    d_pre = (d_active.reshape(mem_local, channels, lat_local, lon_count) * silu_slope(pre)).astype(
        jnp.bfloat16
    )
    dpre_rows = padded(d_pre, (("lat", 2),), 1)
    d_input = (cotangent.astype(jnp.float32) + convolve(dpre_rows, flipped(conv_in))).astype(
        jnp.bfloat16
    )
    grad_in = kernel_grad(ens_rows, d_pre)
    summed = lax.psum((grad_in, grad_pool, grad_out), ("member", "lat"))
    grad_scale = 1.0 / math.sqrt(members * lat_local * lax.axis_size("lat") * lon_count)
    return (
        encoded,
        d_input,
        summed[0] * grad_scale,
        summed[1] * grad_scale,
        summed[2] * grad_scale,
    )


def solution(mesh):
    return jax.shard_map(
        on_device,
        mesh=mesh,
        in_specs=(P("member", None, "lat", None), P("member", None, "lat", None), P(), P(), P()),
        out_specs=(P("member", None, "lat", None), P("member", None, "lat", None), P(), P(), P()),
        check_vma=False,
    )
```

profile of v0, /device:TPU:8, one launch (start us, length us, event | category | flops | bytes accessed | tf_op | source)
XLA Modules:
  0.0 482.6 jit_solution(12388150203696976623)
XLA Ops:
  7.2 1.5 copy.135
  8.9 5.9 %collective-permute-start.1 = (bf16[2,64,1,256]{1,0,3,2:T(2,128)(2,1)S(1)}, bf16[2,64,1,256]{1,0,3,2:T(2,128)(2,1)S(1)}, u32[]{:S(2)}, u32[]{:S(2)}) collective-permute-start(bf16[2,64,1,256]{1,0,3,2:T(2,128)(2,1)S(1)} %get-tuple-element.44), channel_id=1, source_target_pairs={{1,0},{2,1},{3,2},{4,3},{5,4},{6,5},{7,6},{8,7},{9,8},{10,9},{11,1... | collective-permute-start | bytes 196616 | tf_op jit(solution)/shard_map/ppermute | solution.py:18
  14.8 1.9 collective-permute-start
  17.0 6.9 %collective-permute-start.5 = (bf16[2,64,1,256]{3,2,1,0:T(2,128)(2,1)S(1)}, bf16[2,64,1,256]{3,2,1,0:T(2,128)(2,1)S(1)}, u32[]{:S(2)}, u32[]{:S(2)}) collective-permute-start(bf16[2,64,1,256]{3,2,1,0:T(2,128)(2,1)S(1)} %get-tuple-element.46), channel_id=1, source_target_pairs={{1,0},{2,1},{3,2},{4,3},{5,4},{6,5},{7,6},{8,7},{9,8},{10,9},{11,1... | collective-permute-start | bytes 196616 | tf_op jit(solution)/shard_map/ppermute | solution.py:18
  23.9 1.9 collective-permute-start.4
  25.9 8.7 %fusion.81 = bf16[64,6,2,258]{0,2,3,1:T(2,128)(2,1)S(1)} fusion(bf16[2,64,1,256]{1,0,3,2:T(2,128)(2,1)S(1)} %collective-permute-done.1, bf16[2,64,4,256]{1,0,3,2:T(2,128)(2,1)S(1)} %copy.135, bf16[2,64,1,256]{1,0,3,2:T(2,128)(2,1)S(1)} %collective-permute-done), kind=kLoop, calls=%fused_computation.111 | loop fusion | flops 1585152 | bytes 789504 | tf_op jit(solution)/shard_map/concatenate | solution.py:26
  36.2 2.2 add_multiply_fusion
  40.5 8.0 %all-to-all-start = ((bf16[2,128,1024]{1,0,2:T(2,128)(2,1)}), bf16[2,128,1024]{1,0,2:T(2,128)(2,1)S(1)}, u32[]{:S(2)}, u32[]{:S(2)}) async-start(bf16[2,128,1024]{1,0,2:T(2,128)(2,1)} %copy.144), calls=%async_computation | async-start | bytes 1048576 | tf_op jit(solution)/shard_map/all_to_all | solution.py:72
  55.6 9.1 %all-to-all-done = bf16[2,128,1024]{1,0,2:T(2,128)(2,1)S(1)} async-done(((bf16[2,128,1024]{1,0,2:T(2,128)(2,1)}), bf16[2,128,1024]{1,0,2:T(2,128)(2,1)S(1)}, u32[]{:S(2)}, u32[]{:S(2)}) %all-to-all-start) | async-done | bytes 524320 | tf_op jit(solution)/shard_map/all_to_all | solution.py:72
  66.9 15.3 %all_gather.12 = f32[128,1024]{0,1:T(8,128)S(1)} all-gather(f32[128,128]{0,1:T(8,128)S(1)} %convolution_bitcast_fusion.1), channel_id=1, replica_groups=mesh['member'=8,'lat'=32] {'member'}, dimensions={1}, use_global_device_ids=true | all-gather | bytes 589824 | tf_op jit(solution)/shard_map/all_gather | solution.py:80
  84.1 4.1 all-to-all-start.1
  94.4 27.7 %all_gather.15 = f32[128,1024]{0,1:T(8,128)S(1)} all-gather(f32[128,128]{0,1:T(8,128)S(1)} %copy-done.10), channel_id=1, replica_groups=mesh['member'=8,'lat'=32] {'member'}, dimensions={1}, use_global_device_ids=true | all-gather | bytes 589824 | tf_op jit(solution)/shard_map/all_gather | solution.py:81
  122.1 2.0 copy.155
  124.1 2.0 convert_reduce_fusion
  126.1 2.1 copy.165
  129.6 14.9 %all_gather.14 = bf16[128,1024]{0,1:T(8,128)(2,1)S(1)} all-gather(bf16[128,128]{0,1:T(8,128)(2,1)S(1)} %get-tuple-element.48), channel_id=1, replica_groups=mesh['member'=8,'lat'=32] {'member'}, dimensions={1}, use_global_device_ids=true | all-gather | bytes 294912 | tf_op jit(solution)/shard_map/all_gather | solution.py:104
  144.5 14.6 %all_gather.13 = bf16[128,1024]{0,1:T(8,128)(2,1)S(1)} all-gather(bf16[128,128]{0,1:T(8,128)(2,1)S(1)} %get-tuple-element.47), channel_id=1, replica_groups=mesh['member'=8,'lat'=32] {'member'}, dimensions={1}, use_global_device_ids=true | all-gather | bytes 294912 | tf_op jit(solution)/shard_map/all_gather | solution.py:101
  159.2 3.4 fusion.8
  162.8 7.4 %collective-permute-start.3 = (bf16[2,128,1,256]{1,0,3,2:T(2,128)(2,1)S(1)}, bf16[2,128,1,256]{1,0,3,2:T(2,128)(2,1)S(1)}, u32[]{:S(2)}, u32[]{:S(2)}) collective-permute-start(bf16[2,128,1,256]{1,0,3,2:T(2,128)(2,1)S(1)} %get-tuple-element.42), channel_id=1, source_target_pairs={{1,0},{2,1},{3,2},{4,3},{5,4},{6,5},{7,6},{8,7},{9,8},{10,9},{11,1... | collective-permute-start | bytes 393224 | tf_op jit(solution)/shard_map/ppermute | solution.py:18
  170.3 1.9 collective-permute-start.2
  172.4 6.9 %collective-permute-start.7 = (bf16[2,128,1,256]{1,0,3,2:T(2,128)(2,1)S(1)}, bf16[2,128,1,256]{1,0,3,2:T(2,128)(2,1)S(1)}, u32[]{:S(2)}, u32[]{:S(2)}) collective-permute-start(bf16[2,128,1,256]{1,0,3,2:T(2,128)(2,1)S(1)} %get-tuple-element.38), channel_id=1, source_target_pairs={{1,0},{2,1},{3,2},{4,3},{5,4},{6,5},{7,6},{8,7},{9,8},{10,9},{11,1... | collective-permute-start | bytes 393224 | tf_op jit(solution)/shard_map/ppermute | solution.py:18
  179.3 2.1 collective-permute-start.6
  181.4 4.3 fusion.66
  186.8 7.6 %fusion.80 = bf16[128,6,2,258]{0,2,3,1:T(2,128)(2,1)S(1)} fusion(bf16[2,128,1,256]{1,0,3,2:T(2,128)(2,1)S(1)} %collective-permute-done.3, bf16[2,128,4,256]{1,0,3,2:T(2,128)(2,1)S(1)} %get-tuple-element.34, bf16[2,128,1,256]{1,0,3,2:T(2,128)(2,1)S(1)} %collective-permute-done.2), kind=kLoop, calls=%fused_computation.110 | loop fusion | flops 3170304 | bytes 1579008 | tf_op jit(solution)/shard_map/concatenate | solution.py:26
  195.9 1.4 convolution_select_fusion.2
  197.8 7.8 %fusion.43 = bf16[128,6,2,258]{0,2,3,1:T(2,128)(2,1)S(1)} fusion(bf16[2,128,1,256]{1,0,3,2:T(2,128)(2,1)S(1)} %collective-permute-done.7, bf16[2,128,4,256]{1,0,3,2:T(2,128)(2,1)S(1)} %get-tuple-element.33, bf16[2,128,1,256]{1,0,3,2:T(2,128)(2,1)S(1)} %collective-permute-done.6), kind=kLoop, calls=%fused_computation.74 | loop fusion | flops 3170304 | bytes 1579008 | tf_op jit(solution)/shard_map/concatenate | solution.py:26
  207.7 4.1 fusion.67
  211.7 1.4 convolution_select_fusion
  216.5 254.1 %all-reduce.3.cloned.1.call-done = (f32[3,3,64,128]{3,2,1,0:T(8,128)}, f32[256,128]{1,0:T(8,128)}, f32[3,3,128,64]{2,3,1,0:T(8,128)}) async-done(((f32[3,3,64,128]{3,2,1,0:T(8,128)}, f32[256,128]{1,0:T(8,128)}, f32[3,3,128,64]{2,3,1,0:T(8,128)}), (f32[3,3,64,128]{3,2,1,0:T(8,128)}, f32[256,128]{1,0:T(8,128)}, f32[3,3,128,64]{2,3,1,0:T(8,128)})) %all-reduce.3.cloned.1.call-update) | async-done | bytes 720912 | tf_op jit(solution)/shard_map/psum | solution.py:117
  470.6 1.7 broadcast_multiply_fusion.1
  472.3 1.6 broadcast_multiply_fusion.2
  473.9 1.7 broadcast_multiply_fusion
  (121 shorter events, 31.2 us)
Async XLA Ops:
  7.2 28.5 %copy-start = (bf16[3,3,64,128]{3,2,1,0:T(8,128)(2,1)S(1)}, bf16[3,3,64,128]{3,2,1,0:T(8,128)(2,1)}, u32[]{:S(2)}) copy-start(bf16[3,3,64,128]{3,2,1,0:T(8,128)(2,1)} %param.7) | copy-start | bytes 442372
  7.2 9.6 %copy-start.1 = (bf16[2,64,4,256]{3,2,1,0:T(4,128)(2,1)S(1)}, bf16[2,64,4,256]{3,2,1,0:T(4,128)(2,1)}, u32[]{:S(2)}) copy-start(bf16[2,64,4,256]{3,2,1,0:T(4,128)(2,1)} %param.6) | copy-start | bytes 786436
  8.7 25.9 %copy-start.3 = (bf16[2,64,4,256]{1,0,3,2:T(2,128)(2,1)}, bf16[2,64,4,256]{1,0,3,2:T(2,128)(2,1)S(1)}, u32[]{:S(2)}) copy-start(bf16[2,64,4,256]{1,0,3,2:T(2,128)(2,1)S(1)} %copy.135) | copy-start | bytes 786436
  8.9 16.9 %collective-permute-start.1 = (bf16[2,64,1,256]{1,0,3,2:T(2,128)(2,1)S(1)}, bf16[2,64,1,256]{1,0,3,2:T(2,128)(2,1)S(1)}, u32[]{:S(2)}, u32[]{:S(2)}) collective-permute-start(bf16[2,64,1,256]{1,0,3,2:T(2,128)(2,1)S(1)} %get-tuple-element.44), channel_id=1, source_target_pairs={{1,0},{2,1},{3,2},{4,3},{5,4},{6,5},{7,6},{8,7},{9,8},{10,9},{11,1... | collective-permute-start | bytes 196616 | tf_op jit(solution)/shard_map/ppermute | solution.py:18
  14.8 11.0 %collective-permute-start = (bf16[2,64,1,256]{1,0,3,2:T(2,128)(2,1)S(1)}, bf16[2,64,1,256]{1,0,3,2:T(2,128)(2,1)S(1)}, u32[]{:S(2)}, u32[]{:S(2)}) collective-permute-start(bf16[2,64,1,256]{1,0,3,2:T(2,128)(2,1)S(1)} %get-tuple-element.43), channel_id=1, source_target_pairs={{0,1},{1,2},{2,3},{3,4},{4,5},{5,6},{6,7},{7,8},{8,9},{9,10},{10,1... | collective-permute-start | bytes 196616 | tf_op jit(solution)/shard_map/ppermute | solution.py:16
  17.0 31.5 %collective-permute-start.5 = (bf16[2,64,1,256]{3,2,1,0:T(2,128)(2,1)S(1)}, bf16[2,64,1,256]{3,2,1,0:T(2,128)(2,1)S(1)}, u32[]{:S(2)}, u32[]{:S(2)}) collective-permute-start(bf16[2,64,1,256]{3,2,1,0:T(2,128)(2,1)S(1)} %get-tuple-element.46), channel_id=1, source_target_pairs={{1,0},{2,1},{3,2},{4,3},{5,4},{6,5},{7,6},{8,7},{9,8},{10,9},{11,1... | collective-permute-start | bytes 196616 | tf_op jit(solution)/shard_map/ppermute | solution.py:18
  23.9 24.6 %collective-permute-start.4 = (bf16[2,64,1,256]{3,2,1,0:T(2,128)(2,1)S(1)}, bf16[2,64,1,256]{3,2,1,0:T(2,128)(2,1)S(1)}, u32[]{:S(2)}, u32[]{:S(2)}) collective-permute-start(bf16[2,64,1,256]{3,2,1,0:T(2,128)(2,1)S(1)} %get-tuple-element.45), channel_id=1, source_target_pairs={{0,1},{1,2},{2,3},{3,4},{4,5},{5,6},{6,7},{7,8},{8,9},{9,10},{10,1... | collective-permute-start | bytes 196616 | tf_op jit(solution)/shard_map/ppermute | solution.py:16
  25.9 9.6 %copy-start.20 = (bf16[2,64,1,256]{1,0,3,2:T(2,128)(2,1)}, bf16[2,64,1,256]{1,0,3,2:T(2,128)(2,1)S(1)}, u32[]{:S(2)}) copy-start(bf16[2,64,1,256]{1,0,3,2:T(2,128)(2,1)S(1)} %collective-permute-done.1) | copy-start | bytes 196612
  25.9 9.6 %copy-start.22 = (bf16[2,64,1,256]{1,0,3,2:T(2,128)(2,1)}, bf16[2,64,1,256]{1,0,3,2:T(2,128)(2,1)S(1)}, u32[]{:S(2)}) copy-start(bf16[2,64,1,256]{1,0,3,2:T(2,128)(2,1)S(1)} %collective-permute-done) | copy-start | bytes 196612
  40.5 24.2 %all-to-all-start = ((bf16[2,128,1024]{1,0,2:T(2,128)(2,1)}), bf16[2,128,1024]{1,0,2:T(2,128)(2,1)S(1)}, u32[]{:S(2)}, u32[]{:S(2)}) async-start(bf16[2,128,1024]{1,0,2:T(2,128)(2,1)} %copy.144), calls=%async_computation | async-start | bytes 1048576 | tf_op jit(solution)/shard_map/all_to_all | solution.py:72
  64.7 2.0 copy-start.18
  65.2 17.0 %copy-start.9 = (f32[128,128]{0,1:T(8,128)}, f32[128,128]{0,1:T(8,128)S(1)}, u32[]{:S(2)}) copy-start(f32[128,128]{0,1:T(8,128)S(1)} %broadcast_multiply_fusion.3) | copy-start | bytes 196612
  66.0 16.2 %copy-start.15 = (f32[128,128]{0,1:T(8,128)}, f32[128,128]{0,1:T(8,128)S(1)}, u32[]{:S(2)}) copy-start(f32[128,128]{0,1:T(8,128)S(1)} %fusion.13) | copy-start | bytes 196612
  82.7 5.6 %copy-start.12 = (bf16[2,64,4,256]{3,2,1,0:T(4,128)(2,1)S(1)}, bf16[2,64,4,256]{3,2,1,0:T(4,128)(2,1)}, u32[]{:S(2)}) copy-start(bf16[2,64,4,256]{3,2,1,0:T(4,128)(2,1)} %param.5) | copy-start | bytes 786436
  84.1 38.0 %all-to-all-start.1 = ((bf16[2,128,1024]{1,0,2:T(2,128)(2,1)}), bf16[2,128,1024]{1,0,2:T(2,128)(2,1)}, u32[]{:S(2)}, u32[]{:S(2)}) async-start(bf16[2,128,1024]{1,0,2:T(2,128)(2,1)} %copy.154), calls=%async_computation.1 | async-start | bytes 1048576 | tf_op jit(solution)/shard_map/all_to_all | solution.py:94
  88.2 3.4 copy-start.6
  88.2 382.4 %all-reduce.3.cloned.1.call-start = ((), (), s32[]{:S(2)}) async-start(), calls=%async_computation.2 | async-start | bytes 1441792 | tf_op jit(solution)/shard_map/psum | solution.py:117
  91.6 1.2 copy-start.11
  93.3 1.1 copy-start.10
  126.1 3.2 copy-start.19
  126.1 3.4 copy-start.16
  129.6 29.6 %copy-start.2 = (f32[4,2,256,128]{3,0,2,1:T(4,128)S(1)}, f32[4,2,256,128]{3,0,2,1:T(4,128)}, u32[]{:S(2)}) copy-start(f32[4,2,256,128]{3,0,2,1:T(4,128)} %slice.89) | copy-start | bytes 3145732
  159.2 22.2 %copy-start.4 = (bf16[2,64,4,256]{1,0,3,2:T(2,128)(2,1)S(1)}, bf16[2,64,4,256]{1,0,3,2:T(2,128)(2,1)}, u32[]{:S(2)}) copy-start(bf16[2,64,4,256]{1,0,3,2:T(2,128)(2,1)} %copy-done.3) | copy-start | bytes 786436
  159.2 22.2 %copy-start.21 = (bf16[2,64,1,256]{1,0,3,2:T(2,128)(2,1)S(1)}, bf16[2,64,1,256]{1,0,3,2:T(2,128)(2,1)}, u32[]{:S(2)}) copy-start(bf16[2,64,1,256]{1,0,3,2:T(2,128)(2,1)} %copy-done.20) | copy-start | bytes 196612
  159.2 22.2 %copy-start.23 = (bf16[2,64,1,256]{1,0,3,2:T(2,128)(2,1)S(1)}, bf16[2,64,1,256]{1,0,3,2:T(2,128)(2,1)}, u32[]{:S(2)}) copy-start(bf16[2,64,1,256]{1,0,3,2:T(2,128)(2,1)} %copy-done.22) | copy-start | bytes 196612
  162.8 23.9 %collective-permute-start.3 = (bf16[2,128,1,256]{1,0,3,2:T(2,128)(2,1)S(1)}, bf16[2,128,1,256]{1,0,3,2:T(2,128)(2,1)S(1)}, u32[]{:S(2)}, u32[]{:S(2)}) collective-permute-start(bf16[2,128,1,256]{1,0,3,2:T(2,128)(2,1)S(1)} %get-tuple-element.42), channel_id=1, source_target_pairs={{1,0},{2,1},{3,2},{4,3},{5,4},{6,5},{7,6},{8,7},{9,8},{10,9},{11,1... | collective-permute-start | bytes 393224 | tf_op jit(solution)/shard_map/ppermute | solution.py:18
  170.3 16.5 %collective-permute-start.2 = (bf16[2,128,1,256]{1,0,3,2:T(2,128)(2,1)S(1)}, bf16[2,128,1,256]{1,0,3,2:T(2,128)(2,1)S(1)}, u32[]{:S(2)}, u32[]{:S(2)}) collective-permute-start(bf16[2,128,1,256]{1,0,3,2:T(2,128)(2,1)S(1)} %get-tuple-element.41), channel_id=1, source_target_pairs={{0,1},{1,2},{2,3},{3,4},{4,5},{5,6},{6,7},{7,8},{8,9},{9,10},{10,1... | collective-permute-start | bytes 393224 | tf_op jit(solution)/shard_map/ppermute | solution.py:16
  172.4 25.4 %collective-permute-start.7 = (bf16[2,128,1,256]{1,0,3,2:T(2,128)(2,1)S(1)}, bf16[2,128,1,256]{1,0,3,2:T(2,128)(2,1)S(1)}, u32[]{:S(2)}, u32[]{:S(2)}) collective-permute-start(bf16[2,128,1,256]{1,0,3,2:T(2,128)(2,1)S(1)} %get-tuple-element.38), channel_id=1, source_target_pairs={{1,0},{2,1},{3,2},{4,3},{5,4},{6,5},{7,6},{8,7},{9,8},{10,9},{11,1... | collective-permute-start | bytes 393224 | tf_op jit(solution)/shard_map/ppermute | solution.py:18
  179.3 6.4 %copy-start.14 = (f32[128,128]{0,1:T(8,128)S(1)}, f32[128,128]{0,1:T(8,128)}, u32[]{:S(2)}) copy-start(f32[128,128]{0,1:T(8,128)} %copy-done.13) | copy-start | bytes 196612
  179.3 18.5 %collective-permute-start.6 = (bf16[2,128,1,256]{1,0,3,2:T(2,128)(2,1)S(1)}, bf16[2,128,1,256]{1,0,3,2:T(2,128)(2,1)S(1)}, u32[]{:S(2)}, u32[]{:S(2)}) collective-permute-start(bf16[2,128,1,256]{1,0,3,2:T(2,128)(2,1)S(1)} %get-tuple-element.37), channel_id=1, source_target_pairs={{0,1},{1,2},{2,3},{3,4},{4,5},{5,6},{6,7},{7,8},{8,9},{9,10},{10,1... | collective-permute-start | bytes 393224 | tf_op jit(solution)/shard_map/ppermute | solution.py:16
  206.3 1.0 copy-start.8
  206.4 1.2 copy-start.17
  (7 other events, 6.0 us)
Sparse Core Ops, SparseCore 0:
  211.9 258.6 all-reduce.2
where the time goes:
time: 489 us; the launch traced here: 483 us
  waiting for transfers between devices  263 us (54%)
  blocking collectives  72.5 us (15%)
  starting transfers between devices  47.2 us (10%)
  other arithmetic  40.8 us (8%)
  local copies, waits for them, and re-layouts  28.1 us (6%)
  matrix products  15.8 us (3%)
  between operations  15 us (3%)
    psum x1, waiting for transfers between devices, on_device(): summed = lax.psum((grad_in, grad_pool, grad_out), ('member', 'lat'))  254 us
    all_gather x1, blocking collectives, on_device(): lax.all_gather(local_average, 'member', axis=1, tiled=True)  27.7 us
    ppermute x4, starting transfers between devices, padded(): lax.ppermute(head, axis, [((i + 1) % count, i) for i in range(ends)])  27.2 us
    concatenate x4, other arithmetic, wrap_longitude(): return jnp.concatenate([field[..., -1:], field, field[..., :1]], axis=3)  25.5 us
    unnamed x65, local copies, waits for them, and re-layouts  15.6 us
    all_gather x1, blocking collectives, on_device(): lax.all_gather(local_shared, 'member', axis=1, tiled=True)  15.3 us
    all_gather x1, blocking collectives, on_device(): lax.all_gather(coef_spread.astype(jnp.bfloat16), 'member', axis=1, tiled=...  14.9 us
    all_gather x1, blocking collectives, on_device(): lax.all_gather(coef_average.astype(jnp.bfloat16), 'member', axis=1, tiled...  14.6 us
  transfers between devices with their start and end apart: 11, of which 2 were waited for; matrix products, arithmetic and copies ran while one was open for 9% of the time, Pallas kernels for 0%

commit v1 on v0

--- a/solution.py
+++ b/solution.py
@@ -98,9 +98,15 @@
     coef_average = local_dstats[:channels] / members
     coef_spread = local_dstats[channels:] / (members * local_spread)
     coef_average, coef_spread = (
-        lax.all_gather(coef_average.astype(jnp.bfloat16), "member", axis=1, tiled=True).astype(
-            coef_average.dtype
-        ),
+        jnp.concatenate(
+            lax.all_to_all(
+                jnp.stack([coef_average.astype(jnp.bfloat16)] * lax.axis_size("member")),
+                "member",
+                0,
+                0,
+            ),
+            axis=1,
+        ).astype(coef_average.dtype),
         lax.all_gather(coef_spread.astype(jnp.bfloat16), "member", axis=1, tiled=True).astype(
             coef_spread.dtype
         ),

time: 489 us -> 494 us (1.010)
  blocking collectives: 72.5 us -> 50.2 us
  starting transfers between devices: 47.2 us -> 61.4 us
  waiting for transfers between devices: 263 us -> 275 us
    all_gather x1 -> x0, blocking collectives: 14.6 us -> none  [on_device(): lax.all_gather(coef_average.astype(jnp.bfloat16), 'member', axis=1, tiled...]
    all_to_all x1, waiting for transfers between devices: 0.01 us -> 12.1 us  [on_device(): lax.all_to_all(d_zed, 'member', split_axis=2, concat_axis=0, tiled=True)]
    all_to_all x1, starting transfers between devices: 4.14 us -> 15 us  [on_device(): lax.all_to_all(d_zed, 'member', split_axis=2, concat_axis=0, tiled=True)]
    all_gather x1, blocking collectives: 27.7 us -> 20.2 us  [on_device(): lax.all_gather(local_average, 'member', axis=1, tiled=True)]
  transfers between devices with their start and end apart: 11 -> 12, of which waited for: 2 -> 3; matrix products, arithmetic and copies ran while one was open for 9% -> 10% of each run, Pallas kernels for 0% -> 0%
where the time goes in v1:
time: 494 us; the launch traced here: 487 us
  waiting for transfers between devices  275 us (56%)
  starting transfers between devices  61.4 us (12%)
  blocking collectives  50.2 us (10%)
  other arithmetic  42.7 us (9%)
  local copies, waits for them, and re-layouts  27.2 us (6%)
  matrix products  15.7 us (3%)
  between operations  15 us (3%)
    psum x1, waiting for transfers between devices, on_device(): summed = lax.psum((grad_in, grad_pool, grad_out), ('member', 'lat'))  254 us
    ppermute x4, starting transfers between devices, padded(): lax.ppermute(head, axis, [((i + 1) % count, i) for i in range(ends)])  26.6 us
    concatenate x4, other arithmetic, wrap_longitude(): return jnp.concatenate([field[..., -1:], field, field[..., :1]], axis=3)  25.5 us
    all_gather x1, blocking collectives, on_device(): lax.all_gather(local_average, 'member', axis=1, tiled=True)  20.2 us
    all_gather x1, blocking collectives, on_device(): lax.all_gather(local_shared, 'member', axis=1, tiled=True)  15.3 us
    all_to_all x1, starting transfers between devices, on_device(): lax.all_to_all(d_zed, 'member', split_axis=2, concat_axis=0, tiled=True)  15 us
    unnamed x65, local copies, waits for them, and re-layouts  14.9 us
    all_gather x1, blocking collectives, on_device(): lax.all_gather(coef_spread.astype(jnp.bfloat16), 'member', axis=1, tiled=...  14.6 us
  transfers between devices with their start and end apart: 12, of which 3 were waited for; matrix products, arithmetic and copies ran while one was open for 10% of the time, Pallas kernels for 0%

profile of v1, /device:TPU:8, one launch (start us, length us, event | category | flops | bytes accessed | tf_op | source)
XLA Modules:
  0.0 487.3 jit_solution(13540891283059281398)
XLA Ops:
  7.2 1.5 copy.135
  8.9 5.9 %collective-permute-start.1 = (bf16[2,64,1,256]{1,0,3,2:T(2,128)(2,1)S(1)}, bf16[2,64,1,256]{1,0,3,2:T(2,128)(2,1)S(1)}, u32[]{:S(2)}, u32[]{:S(2)}) collective-permute-start(bf16[2,64,1,256]{1,0,3,2:T(2,128)(2,1)S(1)} %get-tuple-element.44), channel_id=1, source_target_pairs={{1,0},{2,1},{3,2},{4,3},{5,4},{6,5},{7,6},{8,7},{9,8},{10,9},{11,1... | collective-permute-start | bytes 196616 | tf_op jit(solution)/shard_map/ppermute | solution.py:18
  14.8 1.9 collective-permute-start
  17.0 6.9 %collective-permute-start.5 = (bf16[2,64,1,256]{3,2,1,0:T(2,128)(2,1)S(1)}, bf16[2,64,1,256]{3,2,1,0:T(2,128)(2,1)S(1)}, u32[]{:S(2)}, u32[]{:S(2)}) collective-permute-start(bf16[2,64,1,256]{3,2,1,0:T(2,128)(2,1)S(1)} %get-tuple-element.46), channel_id=1, source_target_pairs={{1,0},{2,1},{3,2},{4,3},{5,4},{6,5},{7,6},{8,7},{9,8},{10,9},{11,1... | collective-permute-start | bytes 196616 | tf_op jit(solution)/shard_map/ppermute | solution.py:18
  23.9 1.9 collective-permute-start.4
  25.9 8.7 %fusion.81 = bf16[64,6,2,258]{0,2,3,1:T(2,128)(2,1)S(1)} fusion(bf16[2,64,1,256]{1,0,3,2:T(2,128)(2,1)S(1)} %collective-permute-done.1, bf16[2,64,4,256]{1,0,3,2:T(2,128)(2,1)S(1)} %copy.135, bf16[2,64,1,256]{1,0,3,2:T(2,128)(2,1)S(1)} %collective-permute-done), kind=kLoop, calls=%fused_computation.111 | loop fusion | flops 1585152 | bytes 789504 | tf_op jit(solution)/shard_map/concatenate | solution.py:26
  36.2 2.2 add_multiply_fusion
  40.5 8.0 %all-to-all-start = ((bf16[2,128,1024]{1,0,2:T(2,128)(2,1)}), bf16[2,128,1024]{1,0,2:T(2,128)(2,1)S(1)}, u32[]{:S(2)}, u32[]{:S(2)}) async-start(bf16[2,128,1024]{1,0,2:T(2,128)(2,1)} %copy.144), calls=%async_computation | async-start | bytes 1048576 | tf_op jit(solution)/shard_map/all_to_all | solution.py:72
  49.1 1.4 maximum_bitcast_fusion
  55.6 9.1 %all-to-all-done = bf16[2,128,1024]{1,0,2:T(2,128)(2,1)S(1)} async-done(((bf16[2,128,1024]{1,0,2:T(2,128)(2,1)}), bf16[2,128,1024]{1,0,2:T(2,128)(2,1)S(1)}, u32[]{:S(2)}, u32[]{:S(2)}) %all-to-all-start) | async-done | bytes 524320 | tf_op jit(solution)/shard_map/all_to_all | solution.py:72
  67.0 15.3 %all_gather.9 = f32[128,1024]{0,1:T(8,128)S(1)} all-gather(f32[128,128]{0,1:T(8,128)S(1)} %convolution_bitcast_fusion.1), channel_id=1, replica_groups=mesh['member'=8,'lat'=32] {'member'}, dimensions={1}, use_global_device_ids=true | all-gather | bytes 589824 | tf_op jit(solution)/shard_map/all_gather | solution.py:80
  84.1 15.0 %all-to-all-start.1 = ((bf16[2,128,1024]{1,0,2:T(2,128)(2,1)}), bf16[2,128,1024]{1,0,2:T(2,128)(2,1)S(1)}, u32[]{:S(2)}, u32[]{:S(2)}) async-start(bf16[2,128,1024]{1,0,2:T(2,128)(2,1)} %copy.154), calls=%async_computation.1 | async-start | bytes 1048576 | tf_op jit(solution)/shard_map/all_to_all | solution.py:94
  105.3 12.1 %all-to-all-done.1 = bf16[2,128,1024]{1,0,2:T(2,128)(2,1)S(1)} async-done(((bf16[2,128,1024]{1,0,2:T(2,128)(2,1)}), bf16[2,128,1024]{1,0,2:T(2,128)(2,1)S(1)}, u32[]{:S(2)}, u32[]{:S(2)}) %all-to-all-start.1) | async-done | bytes 524320 | tf_op jit(solution)/shard_map/all_to_all | solution.py:94
  118.5 2.0 convert_reduce_fusion
  122.9 4.2 all-to-all-start.2
  127.1 20.2 %all_gather.11 = f32[128,1024]{0,1:T(8,128)S(1)} all-gather(f32[128,128]{0,1:T(8,128)S(1)} %copy-done.10), channel_id=1, replica_groups=mesh['member'=8,'lat'=32] {'member'}, dimensions={1}, use_global_device_ids=true | all-gather | bytes 589824 | tf_op jit(solution)/shard_map/all_gather | solution.py:81
  147.3 14.6 %all_gather.10 = bf16[128,1024]{0,1:T(8,128)(2,1)S(1)} all-gather(bf16[128,128]{0,1:T(8,128)(2,1)S(1)} %get-tuple-element.48), channel_id=1, replica_groups=mesh['member'=8,'lat'=32] {'member'}, dimensions={1}, use_global_device_ids=true | all-gather | bytes 294912 | tf_op jit(solution)/shard_map/all_gather | solution.py:110
  165.0 4.6 fusion.8
  169.7 6.8 %collective-permute-start.3 = (bf16[2,128,1,256]{1,0,3,2:T(2,128)(2,1)S(1)}, bf16[2,128,1,256]{1,0,3,2:T(2,128)(2,1)S(1)}, u32[]{:S(2)}, u32[]{:S(2)}) collective-permute-start(bf16[2,128,1,256]{1,0,3,2:T(2,128)(2,1)S(1)} %get-tuple-element.42), channel_id=1, source_target_pairs={{1,0},{2,1},{3,2},{4,3},{5,4},{6,5},{7,6},{8,7},{9,8},{10,9},{11,1... | collective-permute-start | bytes 393224 | tf_op jit(solution)/shard_map/ppermute | solution.py:18
  176.5 1.9 collective-permute-start.2
  178.7 6.9 %collective-permute-start.7 = (bf16[2,128,1,256]{1,0,3,2:T(2,128)(2,1)S(1)}, bf16[2,128,1,256]{1,0,3,2:T(2,128)(2,1)S(1)}, u32[]{:S(2)}, u32[]{:S(2)}) collective-permute-start(bf16[2,128,1,256]{1,0,3,2:T(2,128)(2,1)S(1)} %get-tuple-element.38), channel_id=1, source_target_pairs={{1,0},{2,1},{3,2},{4,3},{5,4},{6,5},{7,6},{8,7},{9,8},{10,9},{11,1... | collective-permute-start | bytes 393224 | tf_op jit(solution)/shard_map/ppermute | solution.py:18
  185.6 1.9 collective-permute-start.6
  187.6 4.3 fusion.66
  191.8 7.6 %fusion.80 = bf16[128,6,2,258]{0,2,3,1:T(2,128)(2,1)S(1)} fusion(bf16[2,128,1,256]{1,0,3,2:T(2,128)(2,1)S(1)} %collective-permute-done.3, bf16[2,128,4,256]{1,0,3,2:T(2,128)(2,1)S(1)} %get-tuple-element.34, bf16[2,128,1,256]{1,0,3,2:T(2,128)(2,1)S(1)} %collective-permute-done.2), kind=kLoop, calls=%fused_computation.110 | loop fusion | flops 3170304 | bytes 1579008 | tf_op jit(solution)/shard_map/concatenate | solution.py:26
  201.0 1.4 convolution_select_fusion.2
  202.9 7.8 %fusion.43 = bf16[128,6,2,258]{0,2,3,1:T(2,128)(2,1)S(1)} fusion(bf16[2,128,1,256]{1,0,3,2:T(2,128)(2,1)S(1)} %collective-permute-done.7, bf16[2,128,4,256]{1,0,3,2:T(2,128)(2,1)S(1)} %get-tuple-element.33, bf16[2,128,1,256]{1,0,3,2:T(2,128)(2,1)S(1)} %collective-permute-done.6), kind=kLoop, calls=%fused_computation.74 | loop fusion | flops 3170304 | bytes 1579008 | tf_op jit(solution)/shard_map/concatenate | solution.py:26
  212.7 4.0 fusion.67
  216.8 1.4 convolution_select_fusion
  221.5 253.7 %all-reduce.3.cloned.1.call-done = (f32[3,3,64,128]{3,2,1,0:T(8,128)}, f32[256,128]{1,0:T(8,128)}, f32[3,3,128,64]{2,3,1,0:T(8,128)}) async-done(((f32[3,3,64,128]{3,2,1,0:T(8,128)}, f32[256,128]{1,0:T(8,128)}, f32[3,3,128,64]{2,3,1,0:T(8,128)}), (f32[3,3,64,128]{3,2,1,0:T(8,128)}, f32[256,128]{1,0:T(8,128)}, f32[3,3,128,64]{2,3,1,0:T(8,128)})) %all-reduce.3.cloned.1.call-update) | async-done | bytes 720912 | tf_op jit(solution)/shard_map/psum | solution.py:123
  475.3 1.7 broadcast_multiply_fusion.1
  477.0 1.6 broadcast_multiply_fusion.2
  478.5 1.7 broadcast_multiply_fusion
  (123 shorter events, 33.9 us)
Async XLA Ops:
  7.2 28.5 %copy-start = (bf16[3,3,64,128]{3,2,1,0:T(8,128)(2,1)S(1)}, bf16[3,3,64,128]{3,2,1,0:T(8,128)(2,1)}, u32[]{:S(2)}) copy-start(bf16[3,3,64,128]{3,2,1,0:T(8,128)(2,1)} %param.7) | copy-start | bytes 442372
  7.2 9.6 %copy-start.1 = (bf16[2,64,4,256]{3,2,1,0:T(4,128)(2,1)S(1)}, bf16[2,64,4,256]{3,2,1,0:T(4,128)(2,1)}, u32[]{:S(2)}) copy-start(bf16[2,64,4,256]{3,2,1,0:T(4,128)(2,1)} %param.6) | copy-start | bytes 786436
  8.7 25.9 %copy-start.2 = (bf16[2,64,4,256]{1,0,3,2:T(2,128)(2,1)}, bf16[2,64,4,256]{1,0,3,2:T(2,128)(2,1)S(1)}, u32[]{:S(2)}) copy-start(bf16[2,64,4,256]{1,0,3,2:T(2,128)(2,1)S(1)} %copy.135) | copy-start | bytes 786436
  8.9 16.9 %collective-permute-start.1 = (bf16[2,64,1,256]{1,0,3,2:T(2,128)(2,1)S(1)}, bf16[2,64,1,256]{1,0,3,2:T(2,128)(2,1)S(1)}, u32[]{:S(2)}, u32[]{:S(2)}) collective-permute-start(bf16[2,64,1,256]{1,0,3,2:T(2,128)(2,1)S(1)} %get-tuple-element.44), channel_id=1, source_target_pairs={{1,0},{2,1},{3,2},{4,3},{5,4},{6,5},{7,6},{8,7},{9,8},{10,9},{11,1... | collective-permute-start | bytes 196616 | tf_op jit(solution)/shard_map/ppermute | solution.py:18
  14.8 11.0 %collective-permute-start = (bf16[2,64,1,256]{1,0,3,2:T(2,128)(2,1)S(1)}, bf16[2,64,1,256]{1,0,3,2:T(2,128)(2,1)S(1)}, u32[]{:S(2)}, u32[]{:S(2)}) collective-permute-start(bf16[2,64,1,256]{1,0,3,2:T(2,128)(2,1)S(1)} %get-tuple-element.43), channel_id=1, source_target_pairs={{0,1},{1,2},{2,3},{3,4},{4,5},{5,6},{6,7},{7,8},{8,9},{9,10},{10,1... | collective-permute-start | bytes 196616 | tf_op jit(solution)/shard_map/ppermute | solution.py:16
  17.0 31.5 %collective-permute-start.5 = (bf16[2,64,1,256]{3,2,1,0:T(2,128)(2,1)S(1)}, bf16[2,64,1,256]{3,2,1,0:T(2,128)(2,1)S(1)}, u32[]{:S(2)}, u32[]{:S(2)}) collective-permute-start(bf16[2,64,1,256]{3,2,1,0:T(2,128)(2,1)S(1)} %get-tuple-element.46), channel_id=1, source_target_pairs={{1,0},{2,1},{3,2},{4,3},{5,4},{6,5},{7,6},{8,7},{9,8},{10,9},{11,1... | collective-permute-start | bytes 196616 | tf_op jit(solution)/shard_map/ppermute | solution.py:18
  23.9 24.6 %collective-permute-start.4 = (bf16[2,64,1,256]{3,2,1,0:T(2,128)(2,1)S(1)}, bf16[2,64,1,256]{3,2,1,0:T(2,128)(2,1)S(1)}, u32[]{:S(2)}, u32[]{:S(2)}) collective-permute-start(bf16[2,64,1,256]{3,2,1,0:T(2,128)(2,1)S(1)} %get-tuple-element.45), channel_id=1, source_target_pairs={{0,1},{1,2},{2,3},{3,4},{4,5},{5,6},{6,7},{7,8},{8,9},{9,10},{10,1... | collective-permute-start | bytes 196616 | tf_op jit(solution)/shard_map/ppermute | solution.py:16
  25.9 9.6 %copy-start.20 = (bf16[2,64,1,256]{1,0,3,2:T(2,128)(2,1)}, bf16[2,64,1,256]{1,0,3,2:T(2,128)(2,1)S(1)}, u32[]{:S(2)}) copy-start(bf16[2,64,1,256]{1,0,3,2:T(2,128)(2,1)S(1)} %collective-permute-done.1) | copy-start | bytes 196612
  25.9 9.6 %copy-start.22 = (bf16[2,64,1,256]{1,0,3,2:T(2,128)(2,1)}, bf16[2,64,1,256]{1,0,3,2:T(2,128)(2,1)S(1)}, u32[]{:S(2)}) copy-start(bf16[2,64,1,256]{1,0,3,2:T(2,128)(2,1)S(1)} %collective-permute-done) | copy-start | bytes 196612
  40.5 24.2 %all-to-all-start = ((bf16[2,128,1024]{1,0,2:T(2,128)(2,1)}), bf16[2,128,1024]{1,0,2:T(2,128)(2,1)S(1)}, u32[]{:S(2)}, u32[]{:S(2)}) async-start(bf16[2,128,1024]{1,0,2:T(2,128)(2,1)} %copy.144), calls=%async_computation | async-start | bytes 1048576 | tf_op jit(solution)/shard_map/all_to_all | solution.py:72
  64.7 2.0 copy-start.18
  65.3 17.0 %copy-start.9 = (f32[128,128]{0,1:T(8,128)}, f32[128,128]{0,1:T(8,128)S(1)}, u32[]{:S(2)}) copy-start(f32[128,128]{0,1:T(8,128)S(1)} %broadcast_multiply_fusion.3) | copy-start | bytes 196612
  66.1 16.2 %copy-start.15 = (f32[128,128]{0,1:T(8,128)}, f32[128,128]{0,1:T(8,128)S(1)}, u32[]{:S(2)}) copy-start(f32[128,128]{0,1:T(8,128)S(1)} %fusion.13) | copy-start | bytes 196612
  82.7 16.4 %copy-start.12 = (bf16[2,64,4,256]{3,2,1,0:T(4,128)(2,1)S(1)}, bf16[2,64,4,256]{3,2,1,0:T(4,128)(2,1)}, u32[]{:S(2)}) copy-start(bf16[2,64,4,256]{3,2,1,0:T(4,128)(2,1)} %param.5) | copy-start | bytes 786436
  84.1 33.3 %all-to-all-start.1 = ((bf16[2,128,1024]{1,0,2:T(2,128)(2,1)}), bf16[2,128,1024]{1,0,2:T(2,128)(2,1)S(1)}, u32[]{:S(2)}, u32[]{:S(2)}) async-start(bf16[2,128,1024]{1,0,2:T(2,128)(2,1)} %copy.154), calls=%async_computation.1 | async-start | bytes 1048576 | tf_op jit(solution)/shard_map/all_to_all | solution.py:94
  99.1 3.4 copy-start.5
  102.5 1.2 copy-start.11
  120.5 1.3 copy-start.19
  120.5 1.6 copy-start.16
  121.8 5.3 %copy-start.10 = (f32[128,128]{0,1:T(8,128)S(1)}, f32[128,128]{0,1:T(8,128)}, u32[]{:S(2)}) copy-start(f32[128,128]{0,1:T(8,128)} %copy-done.9) | copy-start | bytes 196612
  122.9 39.9 %copy-start.14 = (f32[128,128]{0,1:T(8,128)S(1)}, f32[128,128]{0,1:T(8,128)}, u32[]{:S(2)}) copy-start(f32[128,128]{0,1:T(8,128)} %copy-done.13) | copy-start | bytes 196612
  122.9 41.0 %all-to-all-start.2 = ((bf16[8,128,128]{1,2,0:T(8,128)(2,1)}), bf16[8,128,128]{1,2,0:T(8,128)(2,1)}, u32[]{:S(2)}, u32[]{:S(2)}) async-start(bf16[8,128,128]{1,2,0:T(8,128)(2,1)} %stack.2), calls=%async_computation.2 | async-start | bytes 524288 | tf_op jit(solution)/shard_map/all_to_all | solution.py:102
  127.0 348.2 %all-reduce.3.cloned.1.call-start = ((), (), s32[]{:S(2)}) async-start(), calls=%async_computation.3 | async-start | bytes 1441792 | tf_op jit(solution)/shard_map/psum | solution.py:123
  163.8 1.1 copy-start.6
  165.0 22.6 %copy-start.3 = (bf16[2,64,4,256]{1,0,3,2:T(2,128)(2,1)S(1)}, bf16[2,64,4,256]{1,0,3,2:T(2,128)(2,1)}, u32[]{:S(2)}) copy-start(bf16[2,64,4,256]{1,0,3,2:T(2,128)(2,1)} %copy-done.2) | copy-start | bytes 786436
  165.0 22.6 %copy-start.21 = (bf16[2,64,1,256]{1,0,3,2:T(2,128)(2,1)S(1)}, bf16[2,64,1,256]{1,0,3,2:T(2,128)(2,1)}, u32[]{:S(2)}) copy-start(bf16[2,64,1,256]{1,0,3,2:T(2,128)(2,1)} %copy-done.20) | copy-start | bytes 196612
  165.0 22.6 %copy-start.23 = (bf16[2,64,1,256]{1,0,3,2:T(2,128)(2,1)S(1)}, bf16[2,64,1,256]{1,0,3,2:T(2,128)(2,1)}, u32[]{:S(2)}) copy-start(bf16[2,64,1,256]{1,0,3,2:T(2,128)(2,1)} %copy-done.22) | copy-start | bytes 196612
  169.7 22.1 %collective-permute-start.3 = (bf16[2,128,1,256]{1,0,3,2:T(2,128)(2,1)S(1)}, bf16[2,128,1,256]{1,0,3,2:T(2,128)(2,1)S(1)}, u32[]{:S(2)}, u32[]{:S(2)}) collective-permute-start(bf16[2,128,1,256]{1,0,3,2:T(2,128)(2,1)S(1)} %get-tuple-element.42), channel_id=1, source_target_pairs={{1,0},{2,1},{3,2},{4,3},{5,4},{6,5},{7,6},{8,7},{9,8},{10,9},{11,1... | collective-permute-start | bytes 393224 | tf_op jit(solution)/shard_map/ppermute | solution.py:18
  176.5 15.3 %collective-permute-start.2 = (bf16[2,128,1,256]{1,0,3,2:T(2,128)(2,1)S(1)}, bf16[2,128,1,256]{1,0,3,2:T(2,128)(2,1)S(1)}, u32[]{:S(2)}, u32[]{:S(2)}) collective-permute-start(bf16[2,128,1,256]{1,0,3,2:T(2,128)(2,1)S(1)} %get-tuple-element.41), channel_id=1, source_target_pairs={{0,1},{1,2},{2,3},{3,4},{4,5},{5,6},{6,7},{7,8},{8,9},{9,10},{10,1... | collective-permute-start | bytes 393224 | tf_op jit(solution)/shard_map/ppermute | solution.py:16
  178.7 24.2 %collective-permute-start.7 = (bf16[2,128,1,256]{1,0,3,2:T(2,128)(2,1)S(1)}, bf16[2,128,1,256]{1,0,3,2:T(2,128)(2,1)S(1)}, u32[]{:S(2)}, u32[]{:S(2)}) collective-permute-start(bf16[2,128,1,256]{1,0,3,2:T(2,128)(2,1)S(1)} %get-tuple-element.38), channel_id=1, source_target_pairs={{1,0},{2,1},{3,2},{4,3},{5,4},{6,5},{7,6},{8,7},{9,8},{10,9},{11,1... | collective-permute-start | bytes 393224 | tf_op jit(solution)/shard_map/ppermute | solution.py:18
  185.6 17.3 %collective-permute-start.6 = (bf16[2,128,1,256]{1,0,3,2:T(2,128)(2,1)S(1)}, bf16[2,128,1,256]{1,0,3,2:T(2,128)(2,1)S(1)}, u32[]{:S(2)}, u32[]{:S(2)}) collective-permute-start(bf16[2,128,1,256]{1,0,3,2:T(2,128)(2,1)S(1)} %get-tuple-element.37), channel_id=1, source_target_pairs={{0,1},{1,2},{2,3},{3,4},{4,5},{5,6},{6,7},{7,8},{8,9},{9,10},{10,1... | collective-permute-start | bytes 393224 | tf_op jit(solution)/shard_map/ppermute | solution.py:16
  211.5 1.2 copy-start.17
  (8 other events, 7.0 us)
Sparse Core Ops, SparseCore 0:
  216.9 258.2 all-reduce.2
